TPU v7x, 512 devices: a whole 4x4x16 slice. The times are simulated.
512 devices in a mesh: lon: 8 (over y, core), lat: 16 (over z), depth: 4 (over x).
Axes of the slice: x: 4, y: 4, z: 16, core: 2. Of those that a mesh axis runs over, the one named last changes fastest.
Arguments:
- snapshots: float32 [524288, 256], P(('lon', 'lat', 'depth')), may hold values from -300 to 300
- live_rows: int32 [512], P(('lon', 'lat', 'depth')), may hold values from 128 to 1024, as said below
- column_order: int32 [256], replicated, may hold values from 0 to 255, each once
Outputs:
- snapshot_basis: float32 [524288, 256], P(('lon', 'lat', 'depth'))
- triangular: float32 [256, 256], replicated
- highpass: float32 [524288, 256], P(('lon', 'lat', 'depth'))
Inputs may be any that keep to these rules, and one draw needn't show every extreme that they name: `live_rows`: each entry is a multiple of 128; some block has all 1024 rows live and some other block has 128.
All inputs are finite; a program needn't handle non-finite values.
Results may differ from a plain program's by a relative error of at most 0.00005.
Values sent between devices are 32-bit elements; how exact they have to be, the bound alone decides.
A program may use at most 64 MiB of HBM per device.

v0:
```python
import jax
import jax.numpy as jnp
from jax import lax
from jax.sharding import PartitionSpec as P

LOW = 32


def on_device(snapshots, live_rows, column_order):
    row_count = snapshots.shape[0]
    total_rows = row_count * lax.axis_size("lon") * lax.axis_size("lat") * lax.axis_size("depth")
    picked = jnp.take(snapshots, column_order, axis=1)
    live_mask = (lax.iota(jnp.int32, row_count) < live_rows[0])[:, None]
    masked = jnp.where(live_mask, picked, jnp.zeros_like(picked))
    local_gram = (
        lax.dot_general(masked, masked, (((0,), (0,)), ((), ())), precision=lax.Precision.HIGHEST)
        / total_rows
    )
    global_gram = lax.psum(local_gram, ("lon", "lat", "depth"))
    lower_factor = jnp.linalg.cholesky(global_gram)
    triangular = lower_factor.T
    snapshot_basis = jax.scipy.linalg.solve_triangular(lower_factor, masked.T, lower=True).T
    highpass = masked - jnp.dot(
        snapshot_basis[:, :LOW], triangular[:LOW, :], precision=lax.Precision.HIGHEST
    )
    return (snapshot_basis, triangular, highpass)


def solution(mesh):
    placed = (P(("lon", "lat", "depth"), None), P(("lon", "lat", "depth")), P())
    return jax.shard_map(
        on_device,
        mesh=mesh,
        in_specs=placed,
        out_specs=(P(("lon", "lat", "depth"), None), P(), P(("lon", "lat", "depth"), None)),
        check_vma=False,
    )
```

profile of v0, /device:TPU:2, one launch (start us, length us, event | category | flops | bytes accessed | tf_op | source)
XLA Modules:
  0.0 559.2 jit_solution(3424189647287764068)
XLA Ops:
  7.2 0.0 copy-start.1
  7.2 0.0 all-reduce.3.cloned.1.call-start
  7.2 0.7 compare_select_fusion
  7.9 0.0 copy-done.1
  7.9 1.6 copy.6
  9.5 1.1 gather_fusion
  10.6 0.3 copy.7
  11.6 0.2 select_select_fusion
  11.8 2.5 convolution_multiply_fusion
  14.3 0.0 all-reduce.3.cloned.1.call-update
  14.4 470.3 %all-reduce.3.cloned.1.call-done = f32[256,256]{0,1:T(8,128)} async-done(((f32[256,256]{0,1:T(8,128)}), f32[256,256]{0,1:T(8,128)}) %all-reduce.3.cloned.1.call-update) | async-done | bytes 262160 | tf_op jit(solution)/shard_map/psum | solution.py:19
  484.7 0.0 copy-start
  484.7 1.1 copy.9
  485.8 0.0 copy-done
  485.9 11.7 %cholesky.50 = f32[128,128]{1,0:T(8,128)S(1)} custom-call(f32[128,128]{1,0:T(8,128)S(1)} %cholesky.118), custom_call_target="Cholesky" | custom-call | tf_op jit(solution)/shard_map/jit(cholesky)/cholesky | solution.py:20
  497.7 9.8 %custom-call.15 = f32[1,128,128]{1,2,0:T(8,128)S(1)} custom-call(f32[1,128,128]{2,1,0:T(8,128)S(1)} %get-tuple-element.29), custom_call_target="InvertDiagBlocksLowerTriangular" | custom-call | tf_op jit(solution)/shard_map/jit(cholesky)/cholesky | solution.py:20
  507.5 0.3 fusion.9
  507.8 0.1 copy.10
  507.9 0.3 convolution_subtract_fusion.2
  508.2 11.9 %cholesky.105 = f32[128,128]{1,0:T(8,128)S(1)} custom-call(f32[128,128]{1,0:T(8,128)S(1)} %convolution_subtract_fusion.2), custom_call_target="Cholesky" | custom-call | tf_op jit(solution)/shard_map/jit(cholesky)/cholesky | solution.py:20
  520.1 0.6 compare_reduce_fusion
  522.1 0.1 triangular_solve.60
  522.2 4.0 while.1
  522.2 0.6 fusion.20
  522.8 1.4 bitcast_dynamic-update-slice_fusion.2
  524.2 0.6 fusion.20
  524.8 1.4 bitcast_dynamic-update-slice_fusion.2
  526.2 19.7 %custom-call.16 = f32[2,128,128]{1,2,0:T(8,128)S(1)} custom-call(f32[2,128,128]{2,1,0:T(8,128)S(1)} %get-tuple-element.10), custom_call_target="InvertDiagBlocksLowerTriangular" | custom-call | tf_op jit(solution)/shard_map/jit(_solve_triangular)/triangular_solve | solution.py:22
  545.8 0.6 fusion
  546.5 1.0 convolution_subtract_fusion.1
  547.5 0.6 fusion.8
  548.1 0.1 maximum_bitcast_fusion
  548.2 1.3 copy.11
  549.6 2.0 convolution_subtract_fusion
  551.6 0.8 copy.12
  (14 shorter events, 0.2 us)
Async XLA Ops:
  7.2 0.8 copy-start.1
  7.2 477.5 %all-reduce.3.cloned.1.call-start = ((), (), s32[]{:S(2)}) async-start(), calls=%async_computation | async-start | bytes 524288 | tf_op jit(solution)/shard_map/psum | solution.py:19
  484.7 1.2 copy-start
Sparse Core Ops, SparseCore 0:
  14.5 470.1 all-reduce.2
where the time goes:
time: 559 us
  waiting for transfers between devices  470 us (84%)
  other arithmetic  54.9 us (10%)
  between operations  16.2 us (3%)
  local copies, waits for them, and re-layouts  10.4 us (2%)
  matrix products  7.37 us (1%)
    psum x1, waiting for transfers between devices, on_device(): global_gram = lax.psum(local_gram, ('lon', 'lat', 'depth'))  470 us
    another operation x6, other arithmetic, on_device(): lower_factor = jnp.linalg.cholesky(global_gram)  34.1 us
    another operation x2, other arithmetic, on_device(): jax.scipy.linalg.solve_triangular(lower_factor, masked.T, lower=True)  19.7 us
  transfers between devices with their start and end apart: 1, of which 1 were waited for; matrix products, arithmetic and copies ran while one was open for 0% of the time, Pallas kernels for 0%

commit v1 on v0

--- a/solution.py
+++ b/solution.py
@@ -16,7 +16,9 @@
         lax.dot_general(masked, masked, (((0,), (0,)), ((), ())), precision=lax.Precision.HIGHEST)
         / total_rows
     )
-    global_gram = lax.psum(local_gram, ("lon", "lat", "depth"))
+    global_gram = local_gram
+    for kk in ("lon", ("lat", "depth")):
+        global_gram = jax.lax.psum(global_gram, kk)
     lower_factor = jnp.linalg.cholesky(global_gram)
     triangular = lower_factor.T
     snapshot_basis = jax.scipy.linalg.solve_triangular(lower_factor, masked.T, lower=True).T

time: 559 us -> 439 us (0.79)
  the two profiles are of different devices: /device:TPU:2 before, /device:TPU:8 now
where the time goes in v1:
time: 439 us
  waiting for transfers between devices  349 us (79%)
  other arithmetic  54.7 us (12%)
  between operations  16.2 us (4%)
  local copies, waits for them, and re-layouts  10.4 us (2%)
  matrix products  7.37 us (2%)
    psum x2, waiting for transfers between devices, on_device(): global_gram = jax.lax.psum(global_gram, kk)  349 us
    another operation x6, other arithmetic, on_device(): lower_factor = jnp.linalg.cholesky(global_gram)  33.9 us
    another operation x2, other arithmetic, on_device(): jax.scipy.linalg.solve_triangular(lower_factor, masked.T, lower=True)  19.7 us
  transfers between devices with their start and end apart: 2, of which 2 were waited for; matrix products, arithmetic and copies ran while one was open for 0% of the time, Pallas kernels for 0%

profile of v1, /device:TPU:8, one launch (start us, length us, event | category | flops | bytes accessed | tf_op | source)
XLA Modules:
  0.0 438.5 jit_solution(18401360516119858903)
XLA Ops:
  7.2 0.0 copy-start.1
  7.2 0.0 all-reduce.4.cloned.1.call-start
  7.2 0.7 compare_select_fusion
  7.9 0.0 copy-done.1
  7.9 1.6 copy.6
  9.5 1.1 gather_fusion
  10.6 0.3 copy.7
  11.6 0.2 select_select_fusion
  11.8 2.5 convolution_multiply_fusion
  14.3 0.0 all-reduce.4.cloned.1.call-update
  14.3 0.2 all-reduce.6.cloned.1.call-start
  14.6 77.9 %all-reduce.4.cloned.1.call-done = f32[256,256]{0,1:T(8,128)} async-done(((f32[256,256]{0,1:T(8,128)}), f32[256,256]{0,1:T(8,128)}) %all-reduce.4.cloned.1.call-update) | async-done | bytes 262160 | tf_op jit(solution)/shard_map/psum | solution.py:21
  92.5 0.0 all-reduce.6.cloned.1.call-update
  92.5 271.5 %all-reduce.6.cloned.1.call-done = f32[256,256]{0,1:T(8,128)} async-done(((f32[256,256]{0,1:T(8,128)}), f32[256,256]{0,1:T(8,128)}) %all-reduce.6.cloned.1.call-update) | async-done | bytes 262160 | tf_op jit(solution)/shard_map/psum | solution.py:21
  364.0 0.0 copy-start
  364.0 1.1 copy.9
  365.1 0.0 copy-done
  365.2 11.7 %cholesky.50 = f32[128,128]{1,0:T(8,128)S(1)} custom-call(f32[128,128]{1,0:T(8,128)S(1)} %cholesky.118), custom_call_target="Cholesky" | custom-call | tf_op jit(solution)/shard_map/jit(cholesky)/cholesky | solution.py:22
  376.9 9.8 %custom-call.15 = f32[1,128,128]{1,2,0:T(8,128)S(1)} custom-call(f32[1,128,128]{2,1,0:T(8,128)S(1)} %get-tuple-element.29), custom_call_target="InvertDiagBlocksLowerTriangular" | custom-call | tf_op jit(solution)/shard_map/jit(cholesky)/cholesky | solution.py:22
  386.8 0.3 fusion.9
  387.1 0.1 copy.10
  387.2 0.3 convolution_subtract_fusion.2
  387.5 11.7 %cholesky.105 = f32[128,128]{1,0:T(8,128)S(1)} custom-call(f32[128,128]{1,0:T(8,128)S(1)} %convolution_subtract_fusion.2), custom_call_target="Cholesky" | custom-call | tf_op jit(solution)/shard_map/jit(cholesky)/cholesky | solution.py:22
  399.2 0.6 compare_reduce_fusion
  401.2 0.1 triangular_solve.60
  401.3 4.2 while.1
  401.5 0.6 fusion.20
  402.1 1.4 bitcast_dynamic-update-slice_fusion.2
  403.5 0.6 fusion.20
  404.1 1.4 bitcast_dynamic-update-slice_fusion.2
  405.5 19.7 %custom-call.16 = f32[2,128,128]{1,2,0:T(8,128)S(1)} custom-call(f32[2,128,128]{2,1,0:T(8,128)S(1)} %get-tuple-element.10), custom_call_target="InvertDiagBlocksLowerTriangular" | custom-call | tf_op jit(solution)/shard_map/jit(_solve_triangular)/triangular_solve | solution.py:24
  425.2 0.6 fusion
  425.8 1.0 convolution_subtract_fusion.1
  426.8 0.6 fusion.8
  427.4 0.1 maximum_bitcast_fusion
  427.6 1.3 copy.11
  428.9 2.0 convolution_subtract_fusion
  430.9 0.8 copy.12
  (14 shorter events, 0.2 us)
Async XLA Ops:
  7.2 0.8 copy-start.1
  7.2 85.3 %all-reduce.4.cloned.1.call-start = ((), (), s32[]{:S(2)}) async-start(), calls=%async_computation | async-start | bytes 524288 | tf_op jit(solution)/shard_map/psum | solution.py:21
  14.3 349.6 %all-reduce.6.cloned.1.call-start = ((), (), s32[]{:S(2)}) async-start(), calls=%async_computation.1 | async-start | bytes 524288 | tf_op jit(solution)/shard_map/psum | solution.py:21
  364.0 1.2 copy-start
Sparse Core Ops, SparseCore 0:
  14.5 77.9 all-reduce.3
  95.9 268.0 all-reduce.5
